TPU v7x, 128 devices: a whole 4x4x4 slice. The times are simulated.
128 devices in a mesh: cls: 8 (over y, core), mem: 16 (over z, x).
Axes of the slice: x: 4, y: 4, z: 4, core: 2. Of those that a mesh axis runs over, the one named last changes fastest.
Arguments:
- images: bfloat16 [3072, 65536], P(('cls', 'mem')), may hold values from -6 to 6
- owner_group: int32 [3072, 1], P(('cls', 'mem')), may hold values from 0 to 7; in each aligned block of 24 rows (0 to 23, 24 to 47, ...) at most 6 rows name the same one
- bin_in_group: int32 [3072], P(('cls', 'mem')), may hold values from 0 to 7
- defocus: bfloat16 [3072], P(('cls', 'mem')), may hold values from 0.5 to 2
- projections: bfloat16 [64, 65536], P('cls'), may hold values from -6 to 6
- sketch_weight: bfloat16 [64, 48], replicated, may hold values from -0.875 to 0.875
Outputs:
- basis: bfloat16 [8, 64, 65536], P('cls', None, 'mem')
Inputs may be any that keep to these rules, and one draw needn't show every extreme that they name: `owner_group`: in the particles of one device no class group is named more than 6 times, and 6 is reached on some device.
All inputs are finite; a program needn't handle non-finite values.
Results may differ from a plain program's by a relative error of at most 0.012.
The roundings to bfloat16 on the way count: a program that leaves them out, or rounds other values in their place, can miss the bound.
Values may be sent and summed in bfloat16 or wider, within the bound.
A program may use at most 128 MiB of HBM per device.

v0:
```python
import math
import jax
import jax.numpy as jnp
from jax import lax
from jax.sharding import PartitionSpec as P

SIDE = 256
CAP = 6
HI = lax.Precision.HIGHEST


def wave_slice(first, width):
    position = first + jnp.arange(width, dtype=jnp.int32)
    column = position % SIDE
    row_idx = position // SIDE
    fx = jnp.where(column < SIDE // 2, column, column - SIDE).astype(jnp.float32) / SIDE
    fy = jnp.where(row_idx < SIDE // 2, row_idx, row_idx - SIDE).astype(jnp.float32) / SIDE
    return 160.0 * (fx * fx + fy * fy)


def bmm(a, b):
    return jnp.einsum("nij,njk->nik", a, b, precision=HI)


def coefficients(gram, pixels):
    total = jnp.trace(gram, axis1=1, axis2=2)[:, None, None] + 1e-06
    scaled = gram / total
    ident = jnp.eye(gram.shape[1], dtype=jnp.float32)[None]
    first = 1.5 * ident - 0.5 * scaled
    later = bmm(bmm(first, scaled), first)
    second = 1.5 * ident - 0.5 * later
    return bmm(second, first) * jnp.sqrt(pixels / total)


def tree(gram, n_mem, rank, pixels):
    blocks = n_mem
    k = gram.reshape(n_mem, rank, n_mem, rank)
    chain = None
    while True:
        diag = jnp.stack([k[i, :, i, :] for i in range(blocks)])
        c = coefficients(diag, pixels)
        if chain is None:
            chain = c[:, :, None, :]
        else:
            chain = jnp.einsum("nij,njmk->nimk", c, chain, precision=HI)
        if blocks == 1:
            return chain.reshape(rank, n_mem * rank)
        k = jnp.einsum("aij,ajbk->aibk", c, k, precision=HI)
        k = jnp.einsum("aibk,blk->aibl", k, c, precision=HI)
        half = blocks // 2
        k = k.reshape(half, 2, rank, half, 2, rank).sum(axis=(1, 4))
        chain = (
            chain.reshape(half, 2, rank, -1, rank)
            .transpose(0, 2, 1, 3, 4)
            .reshape(half, rank, -1, rank)
        )
        blocks = half


def body(images, owner_group, bin_in_group, defocus, projections, sketch_weight):
    n_cls = lax.axis_size("cls")
    n_mem = lax.axis_size("mem")
    pixels = images.shape[1]
    width = pixels // n_mem
    member = lax.axis_index("mem")
    cls = lax.axis_index("cls")
    p_dev = images.shape[0]
    bins_here = projections.shape[0]
    rank_k = sketch_weight.shape[0]
    owners = owner_group[:, 0]
    onehot = (owners[:, None] == jnp.arange(n_cls, dtype=jnp.int32)[None, :]).astype(jnp.int32)
    before = jnp.cumsum(onehot, axis=0) - onehot
    rank = jnp.sum(onehot * before, axis=1)
    target = owners * CAP + rank
    meta = jnp.stack(
        [target.astype(jnp.float32), defocus.astype(jnp.float32), bin_in_group.astype(jnp.float32)]
    )
    meta = lax.all_gather(meta, ("cls", "mem"), tiled=False).reshape(n_cls, n_mem, 3, p_dev)
    rows = lax.all_to_all(images, "mem", split_axis=1, concat_axis=0, tiled=True)
    rows = rows.reshape(n_mem, p_dev, width)
    mine = lax.dynamic_index_in_dim(meta, cls, 0, keepdims=False)[:, 0]
    select = jnp.arange(n_cls * CAP, dtype=jnp.float32)[None, :, None] == mine[:, None, :]
    sent = jnp.einsum(
        "mti,mip->mtp", select.astype(jnp.bfloat16), rows, preferred_element_type=jnp.float32
    ).astype(jnp.bfloat16)
    sent = (
        sent.reshape(n_mem, n_cls, CAP, width)
        .transpose(1, 0, 2, 3)
        .reshape(n_cls * n_mem * CAP, width)
    )
    got = lax.all_to_all(sent, "cls", split_axis=0, concat_axis=0, tiled=True)
    slot = (cls * CAP + jnp.arange(CAP, dtype=jnp.int32)).astype(jnp.float32)
    pick = (slot[None, None, :, None] == meta[:, :, None, 0, :]).astype(jnp.float32)
    focus = jnp.sum(pick * meta[:, :, None, 1, :], axis=-1).reshape(-1)
    local_bin = jnp.sum(pick * meta[:, :, None, 2, :], axis=-1)
    valid = jnp.sum(pick, axis=-1)
    bins = jnp.arange(bins_here, dtype=jnp.float32)
    table = jnp.where((local_bin[..., None] == bins) & (valid[..., None] > 0.5), 1.0, 0.0)
    table = table.reshape(-1, bins_here).astype(jnp.bfloat16)
    proj = lax.dynamic_slice_in_dim(projections, member * width, width, 1)
    chosen = jnp.dot(table, proj, preferred_element_type=jnp.float32)
    chi = focus[:, None] * wave_slice(member * width, width)[None, :]
    ctf = -math.sqrt(1.01) * jnp.sin(chi + math.atan(0.1))
    residual = (got.astype(jnp.float32) - ctf * chosen).astype(jnp.bfloat16)
    residual = (
        residual.reshape(n_cls, n_mem, CAP, width)
        .transpose(1, 0, 2, 3)
        .reshape(n_mem, n_cls * CAP, width)
    )
    sketch = jnp.einsum(
        "ks,msp->mkp", sketch_weight, residual, preferred_element_type=jnp.float32
    ).astype(jnp.bfloat16)
    sketch = sketch.reshape(n_mem * rank_k, width)
    gram = jnp.einsum("ap,bp->ab", sketch, sketch, preferred_element_type=jnp.float32)
    gram = lax.psum(gram, "mem")
    coef = tree(gram, n_mem, rank_k, float(pixels)).astype(jnp.bfloat16)
    result = jnp.dot(coef, sketch, preferred_element_type=jnp.float32).astype(jnp.bfloat16)
    return result[None]


def solution(mesh):
    in_specs = (
        P(("cls", "mem"), None),
        P(("cls", "mem"), None),
        P(("cls", "mem")),
        P(("cls", "mem")),
        P("cls", None),
        P(),
    )
    out_specs = P("cls", None, "mem")
    return jax.shard_map(body, mesh=mesh, in_specs=in_specs, out_specs=out_specs, check_vma=False)
```

profile of v0, /device:TPU:1, one launch (start us, length us, event | category | flops | bytes accessed | tf_op | source)
XLA Modules:
  0.0 546.3 jit_solution(17044176956349966713)
XLA Ops:
  6.5 4.0 copy.191
  10.6 8.5 %all-to-all-start = ((bf16[24,16,4096]{2,0,1:T(8,128)(2,1)}), bf16[24,16,4096]{2,0,1:T(8,128)(2,1)}, u32[]{:S(2)}, u32[]{:S(2)}) async-start(bf16[24,16,4096]{2,0,1:T(8,128)(2,1)} %bitcast.266), calls=%async_computation | async-start | bytes 6291456 | tf_op jit(solution)/shard_map/all_to_all | solution.py:79
  19.4 96.3 %all-gather.1 = f32[128,3,24]{2,1,0:T(4,128)S(1)} all-gather(f32[1,3,24]{2,1,0:T(4,128)S(1)} %maximum_bitcast_fusion), channel_id=2, replica_groups=mesh['cls'=8,'mem'=16] {'cls','mem'}, dimensions={0}, use_global_device_ids=true | all-gather | bytes 37152 | tf_op jit(solution)/shard_map/all_gather | solution.py:78
  115.8 3.8 convolution_convert_fusion.1
  119.6 3.4 copy.115
  123.1 3.4 copy.116
  126.5 6.3 %copy.117 = bf16[8,96,4096]{2,1,0:T(8,128)(2,1)} copy(bf16[8,96,4096]{2,0,1:T(8,128)(2,1)S(1)} %bitcast.264) | data formatting | bytes 12582912 | tf_op jit(solution)/shard_map/all_to_all | solution.py:91
  132.8 5.8 %all-to-all-start.1 = ((bf16[8,96,4096]{2,1,0:T(8,128)(2,1)}), bf16[8,96,4096]{2,1,0:T(8,128)(2,1)}, u32[]{:S(2)}, u32[]{:S(2)}) async-start(bf16[8,96,4096]{2,1,0:T(8,128)(2,1)} %copy.117), calls=%async_computation.1 | async-start | bytes 12582912 | tf_op jit(solution)/shard_map/all_to_all | solution.py:91
  138.8 0.4 fusion.22
  140.1 69.9 %all-to-all-done.1 = bf16[8,96,4096]{2,1,0:T(8,128)(2,1)} async-done(((bf16[8,96,4096]{2,1,0:T(8,128)(2,1)}), bf16[8,96,4096]{2,1,0:T(8,128)(2,1)}, u32[]{:S(2)}, u32[]{:S(2)}) %all-to-all-start.1) | async-done | bytes 6291488 | tf_op jit(solution)/shard_map/all_to_all | solution.py:91
  210.0 47.5 %fusion = bf16[768,4096]{1,0:T(8,128)(2,1)} fusion(bf16[768,4096]{1,0:T(8,128)(2,1)} %bitcast.88, f32[4096]{0:T(1024)S(1)} %fusion.85, f32[768]{0:T(1024)S(1)} %mul.219, f32[768]{0:T(1024)S(1)} %eq.134, pred[768]{0:T(1024)(128)(4,1)S(1)} %gt.16, bf16[8,65536]{1,0:T(8,128)(2,1)S(1)} %copy-done, s32[]{:T(128)S(6)} %select_n.80), kind=kOutput, calls=%fused_computation.1 | convolution fusion | flops 72376320 | bytes 12674052 | tf_op jit(solution)/shard_map/dot_general | solution.py:101
  257.5 10.1 %reshape.271 = bf16[8,16,6,4096]{3,2,1,0:T(8,128)(2,1)} reshape(bf16[768,4096]{1,0:T(8,128)(2,1)} %fusion) | data formatting | bytes 12582912 | tf_op jit(solution)/shard_map/reshape | solution.py:106
  267.7 7.0 %copy.125 = bf16[16,8,6,4096]{3,0,2,1:T(8,128)(2,1)S(1)} copy(bf16[16,8,6,4096]{3,2,0,1:T(8,128)(2,1)} %bitcast.261) | data formatting | bytes 12582912 | tf_op jit(solution)/shard_map/transpose | solution.py:107
  274.6 5.7 %convolution_convert_fusion = bf16[16,4096,64]{1,2,0:T(8,128)(2,1)S(1)} fusion(bf16[16,48,4096]{2,0,1:T(8,128)(2,1)S(1)} %bitcast.265, bf16[64,48]{0,1:T(8,128)(2,1)S(1)} %copy-done.4), kind=kOutput, calls=%fused_computation.4 | convolution fusion | flops 406847488 | bytes 14686208 | tf_op jit(solution)/shard_map/ks,msp->mkp/dot_general | solution.py:110
  280.3 3.2 copy-done.2
  283.5 10.8 %fusion.140 = f32[1024,1024]{1,0:T(8,128)} fusion(bf16[1024,4096]{1,0:T(8,128)(2,1)S(1)} %bitcast.259), kind=kOutput, calls=%fused_computation.242 | convolution fusion | flops 8589934592 | bytes 12582912 | tf_op jit(solution)/shard_map/ap,bp->ab/dot_general | solution.py:114
  294.3 7.3 %reshape.274 = f32[16,64,16,64]{3,2,1,0:T(8,128)} reshape(f32[1024,1024]{1,0:T(8,128)} %fusion.140) | data formatting | bytes 8388608 | tf_op jit(solution)/shard_map/reshape | solution.py:37
  301.6 9.2 %copy.127 = f32[16,64,16,64]{3,1,2,0:T(8,128)} copy(f32[16,64,16,64]{3,2,1,0:T(8,128)} %reshape.274) | data formatting | bytes 8388608 | tf_op jit(solution)/shard_map/reshape | solution.py:37
  310.9 139.2 %all-reduce.2.cloned.1.call-done = f32[16,64,16,64]{3,1,2,0:T(8,128)} async-done(((f32[16,64,16,64]{3,1,2,0:T(8,128)}), f32[16,64,16,64]{3,1,2,0:T(8,128)}) %all-reduce.2.cloned.1.call-update) | async-done | bytes 4194320 | tf_op jit(solution)/shard_map/psum | solution.py:115
  450.1 0.9 constant_dynamic-update-slice_fusion.15
  451.0 0.9 constant_dynamic-update-slice_fusion.14
  451.9 1.1 constant_dynamic-update-slice_fusion.13
  453.0 0.8 constant_dynamic-update-slice_fusion.12
  453.7 0.8 constant_dynamic-update-slice_fusion.11
  454.5 0.8 constant_dynamic-update-slice_fusion.10
  455.2 0.8 constant_dynamic-update-slice_fusion.9
  456.0 0.8 constant_dynamic-update-slice_fusion.8
  456.8 0.8 constant_dynamic-update-slice_fusion.7
  457.5 0.8 constant_dynamic-update-slice_fusion.6
  458.3 0.8 constant_dynamic-update-slice_fusion.5
  459.0 0.8 constant_dynamic-update-slice_fusion.4
  459.8 0.8 constant_dynamic-update-slice_fusion.3
  460.6 0.8 constant_dynamic-update-slice_fusion.2
  461.3 0.8 constant_dynamic-update-slice_fusion.1
  462.1 0.8 constant_dynamic-update-slice_fusion
  463.1 0.8 fusion.19
  463.9 0.7 fusion.6
  464.6 0.7 convolution_multiply_fusion
  465.3 8.7 %fusion.1 = f32[16,64,16,64]{3,1,0,2:T(8,128)S(1)} fusion(f32[16,64,16,64]{3,1,2,0:T(8,128)S(1)} %copy-done.3, f32[16,64,64]{2,1,0:T(8,128)S(1)} %convolution_multiply_fusion), kind=kOutput, calls=%fused_computation.2 | convolution fusion | flops 805306368 | bytes 8650752 | tf_op jit(solution)/shard_map/aij,ajbk->aibk/dot_general | solution.py:48
  474.0 26.4 %fusion.16 = f32[16,64,16,64]{3,1,2,0:T(8,128)} fusion(f32[16,64,16,64]{3,1,0,2:T(8,128)S(1)} %fusion.1, f32[16,64,64]{2,1,0:T(8,128)S(1)} %convolution_multiply_fusion), kind=kOutput, calls=%fused_computation.36 | convolution fusion | flops 805306368 | bytes 8650752 | tf_op jit(solution)/shard_map/aibk,blk->aibl/dot_general | solution.py:49
  500.4 4.6 reduce_sum.131
  506.0 0.5 fusion.30
  506.5 0.4 fusion.7
  506.9 0.4 convolution_multiply_fusion.2
  507.4 6.1 %fusion.28 = f32[8,64,8,64]{3,1,0,2:T(8,128)S(1)} fusion(f32[8,64,8,64]{1,3,0,2:T(8,128)S(1)} %reduce_sum.131, f32[8,64,64]{2,1,0:T(8,128)S(1)} %convolution_multiply_fusion.2), kind=kOutput, calls=%fused_computation.53 | convolution fusion | flops 201326592 | bytes 2228224 | tf_op jit(solution)/shard_map/aij,ajbk->aibk/dot_general | solution.py:48
  513.5 1.4 fusion.24
  514.8 6.0 %fusion.26 = f32[8,64,8,64]{3,1,2,0:T(8,128)S(1)} fusion(f32[8,64,8,64]{3,1,0,2:T(8,128)S(1)} %fusion.28, f32[8,64,64]{2,1,0:T(8,128)S(1)} %convolution_multiply_fusion.2), kind=kOutput, calls=%fused_computation.51 | convolution fusion | flops 201326592 | bytes 2228224 | tf_op jit(solution)/shard_map/aibk,blk->aibl/dot_general | solution.py:49
  520.9 0.3 reduce_sum.133
  521.6 0.4 fusion.48
  522.0 0.3 fusion.8
  522.3 0.3 convolution_multiply_fusion.4
  522.7 1.6 fusion.46
  524.3 1.9 fusion.14
  526.2 1.6 fusion.42
  528.2 0.3 fusion.60
  528.5 0.3 fusion.9
  528.7 0.3 convolution_multiply_fusion.6
  529.0 0.5 fusion.44
  529.5 0.6 fusion.12
  530.1 0.3 copy.192
  530.6 0.3 fusion.10
  531.0 0.6 fusion.69
  532.9 0.4 convolution_convert_fusion.3
  533.3 5.7 %fusion.4 = bf16[1,64,4096]{2,1,0:T(8,128)(2,1)} fusion(bf16[64,1024]{1,0:T(8,128)(2,1)S(1)} %convolution_convert_fusion.3, bf16[1024,4096]{1,0:T(8,128)(2,1)} %bitcast.260), kind=kOutput, calls=%fused_computation.8 | convolution fusion | flops 537133056 | bytes 9043968 | tf_op jit(solution)/shard_map/dot_general | solution.py:117
  (79 shorter events, 4.1 us)
Async XLA Ops:
  6.5 203.5 %copy-start = (bf16[8,65536]{1,0:T(8,128)(2,1)S(1)}, bf16[8,65536]{1,0:T(8,128)(2,1)}, u32[]{:S(2)}) copy-start(bf16[8,65536]{1,0:T(8,128)(2,1)} %param.10) | copy-start | bytes 3145732
  6.5 12.5 %copy-start.5 = (s32[24,1]{0,1:T(1,128)S(1)}, s32[24,1]{0,1:T(1,128)}, u32[]{:S(2)}) copy-start(s32[24,1]{0,1:T(1,128)} %param.7) | copy-start | bytes 292
  6.5 12.8 %copy-start.6 = (s32[24]{0:T(128)S(1)}, s32[24]{0:T(128)}, u32[]{:S(2)}) copy-start(s32[24]{0:T(128)} %param.8) | copy-start | bytes 292
  6.5 12.9 %copy-start.7 = (bf16[24]{0:T(256)(128)(2,1)S(1)}, bf16[24]{0:T(256)(128)(2,1)}, u32[]{:S(2)}) copy-start(bf16[24]{0:T(256)(128)(2,1)} %param.9) | copy-start | bytes 148
  10.6 105.2 %all-to-all-start = ((bf16[24,16,4096]{2,0,1:T(8,128)(2,1)}), bf16[24,16,4096]{2,0,1:T(8,128)(2,1)}, u32[]{:S(2)}, u32[]{:S(2)}) async-start(bf16[24,16,4096]{2,0,1:T(8,128)(2,1)} %bitcast.266), calls=%async_computation | async-start | bytes 6291456 | tf_op jit(solution)/shard_map/all_to_all | solution.py:79
  132.8 77.2 %all-to-all-start.1 = ((bf16[8,96,4096]{2,1,0:T(8,128)(2,1)}), bf16[8,96,4096]{2,1,0:T(8,128)(2,1)}, u32[]{:S(2)}, u32[]{:S(2)}) async-start(bf16[8,96,4096]{2,1,0:T(8,128)(2,1)} %copy.117), calls=%async_computation.1 | async-start | bytes 12582912 | tf_op jit(solution)/shard_map/all_to_all | solution.py:91
  138.6 311.4 %all-reduce.2.cloned.1.call-start = ((), (), s32[]{:S(2)}) async-start(), calls=%async_computation.2 | async-start | bytes 16777216 | tf_op jit(solution)/shard_map/psum | solution.py:115
  267.6 7.0 %copy-start.4 = (bf16[64,48]{0,1:T(8,128)(2,1)S(1)}, bf16[64,48]{0,1:T(8,128)(2,1)}, u32[]{:S(2)}) copy-start(bf16[64,48]{0,1:T(8,128)(2,1)} %param.11) | copy-start | bytes 18436
  280.3 3.2 copy-start.2
  450.1 15.3 %copy-start.3 = (f32[16,64,16,64]{3,1,2,0:T(8,128)S(1)}, f32[16,64,16,64]{3,1,2,0:T(8,128)}, u32[]{:S(2)}) copy-start(f32[16,64,16,64]{3,1,2,0:T(8,128)} %all-reduce.2.cloned.1.call-done) | copy-start | bytes 12582916
  530.4 8.6 %copy-start.1 = (bf16[8,65536]{1,0:T(8,128)(2,1)S(1)}, bf16[8,65536]{1,0:T(8,128)(2,1)}, u32[]{:S(2)}) copy-start(bf16[8,65536]{1,0:T(8,128)(2,1)} %param.10) | copy-start | bytes 3145732
Sparse Core Ops, SparseCore 0:
  310.9 139.0 all-reduce.1
where the time goes:
time: 557 us; the launch traced here: 546 us
  waiting for transfers between devices  209 us (38%)
  matrix products  135 us (24%)
  blocking collectives  96.3 us (17%)
  local copies, waits for them, and re-layouts  69.5 us (12%)
  between operations  15.1 us (3%)
  starting transfers between devices  14.3 us (3%)
  other arithmetic  7.06 us (1%)
    psum x1, waiting for transfers between devices, body(): gram = lax.psum(gram, 'mem')  139 us
    all_gather x1, blocking collectives, body(): lax.all_gather(meta, ('cls', 'mem'), tiled=False)  96.3 us
    all_to_all x1, waiting for transfers between devices, body(): got = lax.all_to_all(sent, 'cls', split_axis=0, concat_axis=0, tiled=True)  69.9 us
    dot_general x1, matrix products, body(): chosen = jnp.dot(table, proj, preferred_element_type=jnp.float32)  47.5 us
    dot_general x4, matrix products, tree(): k = jnp.einsum('aibk,blk->aibl', k, c, precision=HI)  34.3 us
    dot_general x4, matrix products, tree(): k = jnp.einsum('aij,ajbk->aibk', c, k, precision=HI)  16.8 us
    reshape x2, local copies, waits for them, and re-layouts, tree(): k = gram.reshape(n_mem, rank, n_mem, rank)  16.5 us
    unnamed x52, local copies, waits for them, and re-layouts  16.4 us
  transfers between devices with their start and end apart: 3, of which 2 were waited for; matrix products, arithmetic and copies ran while one was open for 0% of the time, Pallas kernels for 0%

commit v1 on v0

--- a/solution.py
+++ b/solution.py
@@ -112,7 +112,8 @@
     ).astype(jnp.bfloat16)
     sketch = sketch.reshape(n_mem * rank_k, width)
     gram = jnp.einsum("ap,bp->ab", sketch, sketch, preferred_element_type=jnp.float32)
-    gram = lax.psum(gram, "mem")
+    parts = lax.all_gather(gram, "mem")
+    gram = jnp.sum(parts, axis=0)
     coef = tree(gram, n_mem, rank_k, float(pixels)).astype(jnp.bfloat16)
     result = jnp.dot(coef, sketch, preferred_element_type=jnp.float32).astype(jnp.bfloat16)
     return result[None]

time: 557 us -> 789 us (1.42)
  waiting for transfers between devices: 209 us -> 437 us
  other arithmetic: 7.06 us -> 30 us
  local copies, waits for them, and re-layouts: 69.5 us -> 50.4 us
    all_gather x0 -> x1, waiting for transfers between devices: none -> 367 us  [body(): parts = lax.all_gather(gram, 'mem')]
    psum x1 -> x0, waiting for transfers between devices: 139 us -> none  [body(): gram = lax.psum(gram, 'mem')]
    reduce_sum x0 -> x1, other arithmetic: none -> 22.9 us  [body(): gram = jnp.sum(parts, axis=0)]
    unnamed x52, local copies, waits for them, and re-layouts: 16.4 us -> 4.45 us
    reshape x2 -> x1, local copies, waits for them, and re-layouts: 16.5 us -> 7.24 us  [tree(): k = gram.reshape(n_mem, rank, n_mem, rank)]
where the time goes in v1:
time: 789 us; the launch traced here: 780 us
  waiting for transfers between devices  437 us (55%)
  matrix products  137 us (17%)
  blocking collectives  96.3 us (12%)
  local copies, waits for them, and re-layouts  50.4 us (6%)
  other arithmetic  30 us (4%)
  between operations  15.2 us (2%)
  starting transfers between devices  14.3 us (2%)
    all_gather x1, waiting for transfers between devices, body(): parts = lax.all_gather(gram, 'mem')  367 us
    all_gather x1, blocking collectives, body(): lax.all_gather(meta, ('cls', 'mem'), tiled=False)  96.3 us
    all_to_all x1, waiting for transfers between devices, body(): got = lax.all_to_all(sent, 'cls', split_axis=0, concat_axis=0, tiled=True)  69.9 us
    dot_general x1, matrix products, body(): chosen = jnp.dot(table, proj, preferred_element_type=jnp.float32)  47.5 us
    dot_general x4, matrix products, tree(): k = jnp.einsum('aibk,blk->aibl', k, c, precision=HI)  34.3 us
    reduce_sum x1, other arithmetic, body(): gram = jnp.sum(parts, axis=0)  22.9 us
    dot_general x4, matrix products, tree(): k = jnp.einsum('aij,ajbk->aibk', c, k, precision=HI)  18.9 us
  transfers between devices with their start and end apart: 3, of which 2 were waited for; matrix products, arithmetic and copies ran while one was open for 0% of the time, Pallas kernels for 0%

profile of v1, /device:TPU:1, one launch (start us, length us, event | category | flops | bytes accessed | tf_op | source)
XLA Modules:
  0.0 779.7 jit_solution(6733950433713137099)
XLA Ops:
  6.5 4.0 copy.280
  10.6 8.5 %all-to-all-start = ((bf16[24,16,4096]{2,0,1:T(8,128)(2,1)}), bf16[24,16,4096]{2,0,1:T(8,128)(2,1)}, u32[]{:S(2)}, u32[]{:S(2)}) async-start(bf16[24,16,4096]{2,0,1:T(8,128)(2,1)} %bitcast.251), calls=%async_computation | async-start | bytes 6291456 | tf_op jit(solution)/shard_map/all_to_all | solution.py:79
  19.2 0.2 select_reduce_fusion.4
  19.4 96.3 %all-gather.2 = f32[128,3,24]{2,1,0:T(4,128)S(1)} all-gather(f32[1,3,24]{2,1,0:T(4,128)S(1)} %maximum_bitcast_fusion), channel_id=2, replica_groups=mesh['cls'=8,'mem'=16] {'cls','mem'}, dimensions={0}, use_global_device_ids=true | all-gather | bytes 37152 | tf_op jit(solution)/shard_map/all_gather | solution.py:78
  115.8 3.8 convolution_convert_fusion.1
  119.6 3.4 copy.173
  123.1 3.4 copy.174
  126.5 6.3 copy.175
  132.8 5.8 all-to-all-start.1
  138.6 0.1 fusion.139
  138.8 0.4 fusion.22
  139.2 0.1 copy.180
  139.3 0.1 eq.134
  139.5 0.1 copy.178
  139.6 0.1 mul.219
  139.8 0.1 copy.182
  139.9 0.1 gt.16
  140.1 69.9 %all-to-all-done.1 = bf16[8,96,4096]{2,1,0:T(8,128)(2,1)} async-done(((bf16[8,96,4096]{2,1,0:T(8,128)(2,1)}), bf16[8,96,4096]{2,1,0:T(8,128)(2,1)}, u32[]{:S(2)}, u32[]{:S(2)}) %all-to-all-start.1) | async-done | bytes 6291488 | tf_op jit(solution)/shard_map/all_to_all | solution.py:91
  210.0 47.5 %fusion = bf16[768,4096]{1,0:T(8,128)(2,1)} fusion(bf16[768,4096]{1,0:T(8,128)(2,1)} %bitcast.89, f32[4096]{0:T(1024)S(1)} %fusion.85, f32[768]{0:T(1024)S(1)} %mul.219, f32[768]{0:T(1024)S(1)} %eq.134, pred[768]{0:T(1024)(128)(4,1)S(1)} %gt.16, bf16[8,65536]{1,0:T(8,128)(2,1)S(1)} %copy-done, s32[]{:T(128)S(6)} %select_n.80), kind=kOutput, calls=%fused_computation.1 | convolution fusion | flops 72376320 | bytes 12674052 | tf_op jit(solution)/shard_map/dot_general | solution.py:101
  257.5 10.1 %reshape.271 = bf16[8,16,6,4096]{3,2,1,0:T(8,128)(2,1)} reshape(bf16[768,4096]{1,0:T(8,128)(2,1)} %fusion) | data formatting | bytes 12582912 | tf_op jit(solution)/shard_map/reshape | solution.py:106
  267.7 7.0 copy.183
  274.6 5.7 convolution_convert_fusion
  280.3 3.2 copy-done.3
  283.5 10.8 %fusion.141 = f32[1024,1024]{1,0:T(8,128)} fusion(bf16[1024,4096]{1,0:T(8,128)(2,1)S(1)} %bitcast.244), kind=kOutput, calls=%fused_computation.227 | convolution fusion | flops 8589934592 | bytes 12582912 | tf_op jit(solution)/shard_map/ap,bp->ab/dot_general | solution.py:114
  294.3 366.6 %all-gather.5.cloned.1.call-done = f32[16384,1024]{1,0:T(8,128)} async-done(((f32[1024,1024]{1,0:T(8,128)}), f32[16384,1024]{1,0:T(8,128)}) %all-gather.5.cloned.1.call-update) | async-done | bytes 67108880 | tf_op jit(solution)/shard_map/all_gather | solution.py:115
  661.0 22.9 %reduce_sum.139 = f32[1024,1024]{1,0:T(8,128)} reduce(f32[16,1024,1024]{2,1,0:T(8,128)} %bitcast.22, f32[]{:T(128)} %constant.62.clone.1), dimensions={0}, to_apply=%region_5.6 | reduce | flops 15728640 | bytes 71303168 | tf_op jit(solution)/shard_map/reduce_sum | solution.py:116
  683.9 7.2 reshape.274
  691.1 2.8 fusion.136
  694.2 0.2 select_reduce_fusion
  694.4 0.8 fusion.19
  695.2 0.7 fusion.6
  695.9 0.7 convolution_multiply_fusion
  696.7 10.7 %fusion.1 = f32[16,64,16,64]{3,1,0,2:T(8,128)S(1)} fusion(f32[16,64,16,64]{3,2,1,0:T(8,128)S(1)} %copy-done.2, f32[16,64,64]{2,1,0:T(8,128)S(1)} %convolution_multiply_fusion), kind=kOutput, calls=%fused_computation.2 | convolution fusion | flops 805306368 | bytes 8650752 | tf_op jit(solution)/shard_map/aij,ajbk->aibk/dot_general | solution.py:48
  707.4 26.4 %fusion.16 = f32[16,64,16,64]{3,1,2,0:T(8,128)} fusion(f32[16,64,16,64]{3,1,0,2:T(8,128)S(1)} %fusion.1, f32[16,64,64]{2,1,0:T(8,128)S(1)} %convolution_multiply_fusion), kind=kOutput, calls=%fused_computation.36 | convolution fusion | flops 805306368 | bytes 8650752 | tf_op jit(solution)/shard_map/aibk,blk->aibl/dot_general | solution.py:49
  733.7 4.6 reduce_sum.141
  739.2 0.2 select_reduce_fusion.1
  739.3 0.5 fusion.30
  739.8 0.4 fusion.7
  740.3 0.4 convolution_multiply_fusion.2
  740.7 6.1 fusion.28
  746.8 1.4 fusion.24
  748.2 6.0 fusion.26
  754.2 0.3 reduce_sum.143
  754.9 0.1 select_reduce_fusion.2
  755.0 0.4 fusion.48
  755.4 0.3 fusion.8
  755.7 0.3 convolution_multiply_fusion.4
  756.0 1.6 fusion.46
  757.6 1.9 fusion.14
  759.6 1.6 fusion.42
  761.5 0.3 fusion.60
  761.8 0.3 fusion.9
  762.1 0.3 convolution_multiply_fusion.6
  762.4 0.5 fusion.44
  762.9 0.6 fusion.12
  763.5 0.3 copy.281
  763.8 0.2 dot_general.131
  764.0 0.3 fusion.10
  764.4 0.6 fusion.69
  765.6 0.2 fusion.76
  765.8 0.2 fusion.11
  766.1 0.2 convolution_multiply_fusion.8
  766.3 0.4 convolution_convert_fusion.3
  766.6 5.7 fusion.4
  (80 shorter events, 1.8 us)
Async XLA Ops:
  6.5 203.5 %copy-start = (bf16[8,65536]{1,0:T(8,128)(2,1)S(1)}, bf16[8,65536]{1,0:T(8,128)(2,1)}, u32[]{:S(2)}) copy-start(bf16[8,65536]{1,0:T(8,128)(2,1)} %param.10) | copy-start | bytes 3145732
  6.5 12.5 %copy-start.5 = (s32[24,1]{0,1:T(1,128)S(1)}, s32[24,1]{0,1:T(1,128)}, u32[]{:S(2)}) copy-start(s32[24,1]{0,1:T(1,128)} %param.7) | copy-start | bytes 292
  6.5 12.8 %copy-start.6 = (bf16[24]{0:T(256)(128)(2,1)S(1)}, bf16[24]{0:T(256)(128)(2,1)}, u32[]{:S(2)}) copy-start(bf16[24]{0:T(256)(128)(2,1)} %param.9) | copy-start | bytes 148
  6.5 12.9 %copy-start.7 = (s32[24]{0:T(128)S(1)}, s32[24]{0:T(128)}, u32[]{:S(2)}) copy-start(s32[24]{0:T(128)} %param.8) | copy-start | bytes 292
  10.6 105.2 %all-to-all-start = ((bf16[24,16,4096]{2,0,1:T(8,128)(2,1)}), bf16[24,16,4096]{2,0,1:T(8,128)(2,1)}, u32[]{:S(2)}, u32[]{:S(2)}) async-start(bf16[24,16,4096]{2,0,1:T(8,128)(2,1)} %bitcast.251), calls=%async_computation | async-start | bytes 6291456 | tf_op jit(solution)/shard_map/all_to_all | solution.py:79
  132.8 77.2 %all-to-all-start.1 = ((bf16[8,96,4096]{2,1,0:T(8,128)(2,1)}), bf16[8,96,4096]{2,1,0:T(8,128)(2,1)}, u32[]{:S(2)}, u32[]{:S(2)}) async-start(bf16[8,96,4096]{2,1,0:T(8,128)(2,1)} %copy.175), calls=%async_computation.1 | async-start | bytes 12582912 | tf_op jit(solution)/shard_map/all_to_all | solution.py:91
  138.6 522.4 %all-gather.5.cloned.1.call-start = ((), (), s32[]{:S(2)}) async-start(), calls=%async_computation.2 | async-start | bytes 71303168 | tf_op jit(solution)/shard_map/all_gather | solution.py:115
  267.6 7.0 copy-start.4
  280.3 3.2 copy-start.3
  691.1 5.5 copy-start.2
  763.8 8.6 %copy-start.1 = (bf16[8,65536]{1,0:T(8,128)(2,1)S(1)}, bf16[8,65536]{1,0:T(8,128)(2,1)}, u32[]{:S(2)}) copy-start(bf16[8,65536]{1,0:T(8,128)(2,1)} %param.10) | copy-start | bytes 3145732
Sparse Core Ops, SparseCore 0:
  294.4 366.5 all-gather.4
